TPU v7x, 512 devices: a whole 4x8x8 slice. The times are simulated.
512 devices in a mesh: tensor: 64 (over x, y, core), replica: 8 (over z).
Axes of the slice: x: 4, y: 8, z: 8, core: 2. Of those that a mesh axis runs over, the one named last changes fastest.
Arguments:
- amplitudes: bfloat16 [1024, 64, 128], P('tensor'), may hold values from -6 to 6
- block_slot: int32 [1024], replicated, may hold values from 0 to 1023, each once
- integrals: bfloat16 [1024, 64, 64, 64], P('tensor', 'replica'), may hold values from -0.09375 to 0.09375
- tile_cols: int32 [1024, 64], P('tensor'), may hold values from 0 to 1023, as said below
- irreps: int32 [1024], replicated, may hold values from 0 to 7, as said below
Outputs:
- ladder: float32 [1024, 64, 128], P('tensor', None, 'replica')
Inputs may be any that keep to these rules, and one draw needn't show every extreme that they name: `block_slot`: each block has one slot and each slot one block. `tile_cols`: the tiles of a row that name blocks of the row's own irrep name distinct blocks; other tiles may name any block of another irrep. `irreps`: each irrep labels exactly 128 blocks.
All inputs are finite; a program needn't handle non-finite values.
Results may differ from a plain program's by a relative error of at most 0.0003.
Values may be sent and summed in bfloat16 or wider, within the bound.
No kernel may reach another device: no remote copies, remote signals or barrier semaphores. Data moves between devices by JAX's collectives and lax.ppermute only.
A program may use at most 128 MiB of HBM per device.

v0:
```python
import jax
import jax.numpy as jnp
from jax import lax
from jax.sharding import PartitionSpec as P


def local(amplitudes, block_slot, integrals, tile_cols, irreps):
    blocks = tile_cols.shape[0]
    rep_id = lax.axis_index("replica")
    rows_glob = lax.axis_index("tensor") * blocks + jnp.arange(blocks, dtype=jnp.int32)
    row_irrep = irreps[rows_glob]
    per_rep = integrals.shape[1]
    my_cols = lax.dynamic_slice_in_dim(tile_cols, rep_id * per_rep, per_rep, 1)
    whole = lax.all_gather(amplitudes, "tensor", axis=0, tiled=True)
    picked = whole[block_slot[my_cols]]
    allowed = (irreps[my_cols] == row_irrep[:, None]).astype(jnp.bfloat16)
    tiles = integrals * allowed[:, :, None, None]
    partial_sum = jnp.einsum("bnxy,bnyp->bxp", tiles, picked, preferred_element_type=jnp.float32)
    return lax.psum_scatter(partial_sum, "replica", scatter_dimension=2, tiled=True)


def solution(mesh):
    in_specs = (
        P("tensor", None, None),
        P(),
        P("tensor", "replica", None, None),
        P("tensor", None),
        P(),
    )
    out_specs = P("tensor", None, "replica")
    return jax.shard_map(local, mesh=mesh, in_specs=in_specs, out_specs=out_specs, check_vma=False)
```

profile of v0, /device:TPU:2, one launch (start us, length us, event | category | flops | bytes accessed | tf_op | source)
XLA Modules:
  0.0 177.6 jit_solution(1262501762788884398)
XLA Ops:
  6.5 0.0 copy-start
  6.5 0.0 all-gather.2.cloned.1.call-start
  6.5 0.7 all-gather.2.cloned.1.call-update
  7.3 0.0 reduce-scatter.2.cloned.1.call-start
  7.3 0.8 compare_select_fusion.1
  8.1 0.1 reshape.50
  8.2 0.0 copy-done
  8.2 0.6 gather_fusion.1
  8.9 0.0 copy-start.1
  8.9 1.0 gather_fusion
  9.9 0.0 copy-done.1
  9.9 1.0 gather_fusion.2
  10.8 0.1 reshape.49
  10.9 0.1 gather.17
  11.0 0.1 reshape.74
  11.1 0.1 compare_convert_fusion
  11.2 107.2 %all-gather.2.cloned.1.call-done = bf16[1024,64,128]{2,1,0:T(8,128)(2,1)} async-done(((bf16[16,64,128]{2,1,0:T(8,128)(2,1)}), bf16[1024,64,128]{2,1,0:T(8,128)(2,1)}) %all-gather.2.cloned.1.call-update) | async-done | bytes 16777232 | tf_op jit(solution)/shard_map/all_gather | solution.py:14
  118.4 6.7 %gather_fusion.3 = bf16[128,64,128]{2,1,0:T(8,128)(2,1)S(1)} fusion(bf16[1024,64,128]{2,1,0:T(8,128)(2,1)} %all-gather.2.cloned.1.call-done, s32[1024]{0:T(1024)S(1)} %pad_clamp_fusion), kind=kCustom, calls=%fused_computation.3 | custom fusion | bytes 4194816 | tf_op jit(solution)/shard_map/gather | solution.py:15
  125.2 4.1 %fusion.2 = f32[16,64,128]{1,2,0:T(8,128)} fusion(bf16[16,8,64,128]{3,2,1,0:T(8,128)(2,1)S(1)} %bitcast.9, bf16[16,8,64,64]{3,2,1,0:T(8,128)(2,1)} %param.7, bf16[16,8]{1,0:T(8,128)(2,1)S(1)} %compare_convert_fusion), kind=kOutput, calls=%fused_computation.6 | convolution fusion | flops 134742016 | bytes 3670272 | tf_op jit(solution)/shard_map/bnxy,bnyp->bxp/dot_general | solution.py:18
  129.3 0.0 reduce-scatter.2.cloned.1.call-update
  129.3 41.4 %reduce-scatter.2.cloned.1.call-done = f32[16,64,16]{1,2,0:T(8,128)} async-done(((f32[16,64,128]{1,2,0:T(8,128)}), f32[16,64,16]{1,2,0:T(8,128)}) %reduce-scatter.2.cloned.1.call-update) | async-done | bytes 65552 | tf_op jit(solution)/shard_map/reduce_scatter | solution.py:19
  (5 shorter events, 0.0 us)
Async XLA Ops:
  6.5 1.7 copy-start
  6.5 111.9 %all-gather.2.cloned.1.call-start = ((), (), s32[]{:S(2)}) async-start(), calls=%async_computation.1 | async-start | bytes 17039360 | tf_op jit(solution)/shard_map/all_gather | solution.py:14
  7.3 163.5 %reduce-scatter.2.cloned.1.call-start = ((), (), s32[]{:S(2)}) async-start(), calls=%async_computation.2 | async-start | bytes 1179648 | tf_op jit(solution)/shard_map/reduce_scatter | solution.py:19
  8.9 1.0 copy-start.1
Sparse Core Ops, SparseCore 0:
  10.7 107.6 all-gather.1
  129.4 41.2 reduce-scatter.1
where the time goes:
time: 178 us
  waiting for transfers between devices  149 us (84%)
  between operations  13.5 us (8%)
  local copies, waits for them, and re-layouts  9.65 us (5%)
  matrix products  4.12 us (2%)
    all_gather x1, waiting for transfers between devices, local(): whole = lax.all_gather(amplitudes, 'tensor', axis=0, tiled=True)  107 us
    reduce_scatter x1, waiting for transfers between devices, local(): lax.psum_scatter(partial_sum, 'replica', scatter_dimension=2, tiled=True)  41.4 us
    gather x3, local copies, waits for them, and re-layouts, local(): picked = whole[block_slot[my_cols]]  7.77 us
    dot_general x1, matrix products, local(): jnp.einsum('bnxy,bnyp->bxp', tiles, picked, preferred_element_type=jnp.fl...  4.12 us
  transfers between devices with their start and end apart: 2, of which 2 were waited for; matrix products, arithmetic and copies ran while one was open for 2% of the time, Pallas kernels for 0%

commit v1 on v0

--- a/solution.py
+++ b/solution.py
@@ -1,7 +1,20 @@
+import functools
 import jax
 import jax.numpy as jnp
 from jax import lax
 from jax.sharding import PartitionSpec as P
+
+
+def pass_table_here(own_rows, device_axis):
+    store = []
+    amount_of = lax.psum(1, device_axis)
+    for u in range(own_rows.ndim):
+        store.append(amount_of if u == 0 else 1)
+    block_next = jnp.tile(own_rows, store)
+    return lax.all_to_all(block_next, device_axis, split_axis=0, concat_axis=0, tiled=True)
+
+
+assign_the_orders = functools.partial(pass_table_here, device_axis="tensor")
 
 
 def local(amplitudes, block_slot, integrals, tile_cols, irreps):
@@ -11,7 +24,7 @@
     row_irrep = irreps[rows_glob]
     per_rep = integrals.shape[1]
     my_cols = lax.dynamic_slice_in_dim(tile_cols, rep_id * per_rep, per_rep, 1)
-    whole = lax.all_gather(amplitudes, "tensor", axis=0, tiled=True)
+    whole = assign_the_orders(amplitudes)
     picked = whole[block_slot[my_cols]]
     allowed = (irreps[my_cols] == row_irrep[:, None]).astype(jnp.bfloat16)
     tiles = integrals * allowed[:, :, None, None]

time: 178 us -> 451 us (2.53)
  the two profiles are of different devices: /device:TPU:2 before, /device:TPU:4 now
where the time goes in v1:
time: 451 us; the launch traced here: 450 us
  waiting for transfers between devices  404 us (90%)
  local copies, waits for them, and re-layouts  17 us (4%)
  between operations  13.5 us (3%)
  starting transfers between devices  11.5 us (3%)
    all_to_all x1, waiting for transfers between devices, pass_table_here(): lax.all_to_all(block_next, device_axis, split_axis=0, concat_axis=0, tile...  358 us
    reduce_scatter x1, waiting for transfers between devices, local(): lax.psum_scatter(partial_sum, 'replica', scatter_dimension=2, tiled=True)  45.4 us
    all_to_all x1, starting transfers between devices, pass_table_here(): lax.all_to_all(block_next, device_axis, split_axis=0, concat_axis=0, tile...  11.4 us
  transfers between devices with their start and end apart: 2, of which 2 were waited for; matrix products, arithmetic and copies ran while one was open for 1% of the time, Pallas kernels for 0%

profile of v1, /device:TPU:4, one launch (start us, length us, event | category | flops | bytes accessed | tf_op | source)
XLA Modules:
  0.0 450.2 jit_solution(12165860627065780339)
XLA Ops:
  6.5 0.0 copy-start
  6.5 6.9 %tile.4 = bf16[64,16,64,128]{3,2,1,0:T(8,128)(2,1)} broadcast(bf16[16,64,128]{2,1,0:T(8,128)(2,1)} %param.5), dimensions={1,2,3} | broadcast | bytes 17039360 | tf_op jit(solution)/shard_map/tile | solution.py:13
  13.5 0.0 copy-start.2
  13.5 11.4 %all-to-all-start = ((bf16[1024,64,128]{2,1,0:T(8,128)(2,1)}), bf16[1024,64,128]{2,1,0:T(8,128)(2,1)}, u32[]{:S(2)}, u32[]{:S(2)}) async-start(bf16[1024,64,128]{2,1,0:T(8,128)(2,1)} %bitcast.10), calls=%async_computation | async-start | bytes 33554432 | tf_op jit(solution)/shard_map/all_to_all | solution.py:14
  24.9 0.0 copy-start.1
  24.9 0.0 reduce-scatter.2.cloned.1.call-start
  25.0 0.0 copy-done.2
  25.0 0.1 compare_select_fusion.1
  25.1 0.1 reshape.54
  25.2 0.4 copy-done.1
  25.6 1.0 gather_fusion.2
  26.6 0.1 gather.17
  26.7 0.1 reshape.78
  26.8 0.0 copy-done
  26.8 1.0 gather_fusion
  27.8 0.1 reshape.53
  27.9 0.6 gather_fusion.1
  28.5 0.1 compare_convert_fusion
  28.6 358.5 %all-to-all-done = bf16[1024,64,128]{2,1,0:T(8,128)(2,1)} async-done(((bf16[1024,64,128]{2,1,0:T(8,128)(2,1)}), bf16[1024,64,128]{2,1,0:T(8,128)(2,1)}, u32[]{:S(2)}, u32[]{:S(2)}) %all-to-all-start) | async-done | bytes 16777248 | tf_op jit(solution)/shard_map/all_to_all | solution.py:14
  387.1 6.7 %gather_fusion.3 = bf16[128,64,128]{2,1,0:T(8,128)(2,1)S(1)} fusion(bf16[1024,64,128]{2,1,0:T(8,128)(2,1)} %all-to-all-done, s32[1024]{0:T(1024)S(1)} %pad_clamp_fusion), kind=kCustom, calls=%fused_computation.3 | custom fusion | bytes 4194816 | tf_op jit(solution)/shard_map/gather | solution.py:28
  393.8 4.1 fusion.2
  397.9 0.0 reduce-scatter.2.cloned.1.call-update
  397.9 45.4 %reduce-scatter.2.cloned.1.call-done = f32[16,64,16]{1,2,0:T(8,128)} async-done(((f32[16,64,128]{1,2,0:T(8,128)}), f32[16,64,16]{1,2,0:T(8,128)}) %reduce-scatter.2.cloned.1.call-update) | async-done | bytes 65552 | tf_op jit(solution)/shard_map/reduce_scatter | solution.py:32
  (5 shorter events, 0.0 us)
Async XLA Ops:
  6.5 20.2 %copy-start = (s32[1024]{0:T(1024)S(1)}, s32[1024]{0:T(1024)}, u32[]{:S(2)}) copy-start(s32[1024]{0:T(1024)} %param.9) | copy-start | bytes 12292
  13.5 11.5 %copy-start.2 = (s32[16,64]{1,0:T(8,128)S(1)}, s32[16,64]{1,0:T(8,128)}, u32[]{:S(2)}) copy-start(s32[16,64]{1,0:T(8,128)} %param.8) | copy-start | bytes 12292
  13.5 373.6 %all-to-all-start = ((bf16[1024,64,128]{2,1,0:T(8,128)(2,1)}), bf16[1024,64,128]{2,1,0:T(8,128)(2,1)}, u32[]{:S(2)}, u32[]{:S(2)}) async-start(bf16[1024,64,128]{2,1,0:T(8,128)(2,1)} %bitcast.10), calls=%async_computation | async-start | bytes 33554432 | tf_op jit(solution)/shard_map/all_to_all | solution.py:14
  24.9 0.7 copy-start.1
  24.9 418.4 %reduce-scatter.2.cloned.1.call-start = ((), (), s32[]{:S(2)}) async-start(), calls=%async_computation.2 | async-start | bytes 1179648 | tf_op jit(solution)/shard_map/reduce_scatter | solution.py:32
Sparse Core Ops, SparseCore 0:
  398.1 45.2 reduce-scatter.1
